TPU v7x, 256 devices: a whole 4x4x8 slice. The times are simulated.
256 devices in a mesh: area: 32 (over y, x, core), pop: 8 (over z).
Axes of the slice: x: 4, y: 4, z: 8, core: 2. Of those that a mesh axis runs over, the one named last changes fastest.
Arguments:
- history: bfloat16 [4, 32, 64, 32, 128], P(None, 'area', 'pop'), may hold values from -1 to 1
- external: bfloat16 [32, 64, 32, 128], P('area', 'pop'), may hold values from -6 to 6
- leak_rate: float32 [32, 64, 128], P('area', 'pop'), may hold values from 0.05 to 1
- intra_index: int32 [32, 64, 32], P('area', 'pop'), may hold values from 0 to 63
- intra_weight: bfloat16 [32, 64, 32, 128, 128], P('area', 'pop'), may hold values from -0.09375 to 0.09375
- inter_pick: int32 [32, 64, 12], P('area', 'pop'), may hold values from 0 to 1
- inter_weight: bfloat16 [32, 64, 12, 128, 128], P('area', 'pop'), may hold values from -0.15625 to 0.15625
- source_area: int32 [32, 12], replicated, may hold values from 0 to 31, as said below
- delays: int32 [32, 12], replicated, may hold values from 1 to 3
- live_blocks: int32 [32], replicated, may hold values from 8 to 64, as said below
Outputs:
- activity: float32 [32, 64, 32, 128], P('area', 'pop')
Inputs may be any that keep to these rules, and one draw needn't show every extreme that they name: `source_area`: the 12 source areas of an area are distinct and differ from the area itself. `live_blocks`: some area is fully populated and some has 8 populated blocks.
All inputs are finite; a program needn't handle non-finite values.
Results may differ from a plain program's by a relative error of at most 0.0014.
Values may be sent and summed in bfloat16 or wider, within the bound.
No kernel may reach another device: no remote copies, remote signals or barrier semaphores. Data moves between devices by JAX's collectives and lax.ppermute only.
A program may use at most 64 MiB of HBM per device.

v0:
```python
import jax
import jax.numpy as jnp
from jax import lax
from jax.sharding import PartitionSpec as P

SEND_DEV = 2
STEPS = 10


def shards(
    history,
    external,
    leak_rate,
    intra_index,
    intra_weight,
    inter_pick,
    inter_weight,
    source_area,
    delays,
    live_blocks,
):
    area_pos = lax.axis_index("area")
    pop_pos = lax.axis_index("pop")
    blk_local = history.shape[2]
    edge_count = inter_pick.shape[2]
    block_ids = pop_pos * blk_local + jnp.arange(blk_local, dtype=jnp.int32)
    alive_mask = (block_ids < live_blocks[area_pos]).astype(jnp.float32)[:, None, None]
    own_hist = (history[:, 0].astype(jnp.float32) * alive_mask[None]).astype(jnp.bfloat16)
    activity = own_hist[0].astype(jnp.float32)
    my_source = source_area[area_pos]
    tile_index = intra_index[0]
    w_inner = intra_weight[0]
    w_outer = inter_weight[0]
    flat_pick = jnp.arange(edge_count, dtype=jnp.int32)[None, :] * SEND_DEV + inter_pick[0]
    leak_cells = leak_rate[0][:, None, :]
    drive_ext = external[0].astype(jnp.float32)

    def advance(activity, rate_now, edge_rows):
        area_rates = lax.all_gather(rate_now, "pop", axis=0, tiled=True)
        tile_rows = jnp.take(area_rates, tile_index, axis=0)
        inner_term = jnp.einsum(
            "rkji,rktj->rti", w_inner, tile_rows, preferred_element_type=jnp.float32
        )
        flat_rows = edge_rows.reshape((edge_count * SEND_DEV,) + edge_rows.shape[2:])
        source_rows = jnp.take(flat_rows, flat_pick, axis=0)
        outer_term = jnp.einsum(
            "rkji,rktj->rti", w_outer, source_rows, preferred_element_type=jnp.float32
        )
        drive_term = jnp.tanh(inner_term + outer_term + drive_ext)
        return alive_mask * ((1.0 - leak_cells) * activity + leak_cells * drive_term)

    delay_to = jnp.sum(jnp.where(source_area == area_pos, delays, 0), axis=1)
    edge_flag = (delay_to > 0).astype(jnp.bfloat16)[:, None, None, None]

    def turn_slots(position, carried):
        activity, sent_hist, rate_now = carried
        chosen = jnp.take(sent_hist, delay_to, axis=0) * edge_flag
        received = lax.all_to_all(chosen, "area", split_axis=0, concat_axis=0, tiled=True)
        edge_rows = jnp.take(received, my_source, axis=0)
        activity = advance(activity, rate_now, edge_rows)
        rate_now = activity.astype(jnp.bfloat16)
        sent_hist = jnp.concatenate([rate_now[None, :SEND_DEV], sent_hist[:-1]], 0)
        return (activity, sent_hist, rate_now)

    activity, sent_hist, rate_now = lax.fori_loop(
        0, STEPS, turn_slots, (activity, own_hist[:, :SEND_DEV], own_hist[0])
    )
    return activity[None]


def solution(mesh):
    placed = (
        P(None, "area", "pop", None, None),
        P("area", "pop", None, None),
        P("area", "pop", None),
        P("area", "pop", None),
        P("area", "pop", None, None, None),
        P("area", "pop", None),
        P("area", "pop", None, None, None),
        P(),
        P(),
        P(),
    )
    return jax.shard_map(
        shards, mesh=mesh, in_specs=placed, out_specs=P("area", "pop", None, None), check_vma=False
    )
```

profile of v0, /device:TPU:4, one launch (start us, length us, event | category | flops | bytes accessed | tf_op | source)
XLA Modules:
  0.0 475.0 jit_solution(8111666128941133246)
XLA Ops:
  0.0 1.3 dynamic_slice.6
  1.9 1.1 fusion.23
  3.0 1.5 slice_bitcast_fusion.1
  6.8 467.5 %while.15 = (s32[]{:T(128)}, f32[8,32,128]{2,1,0:T(8,128)S(1)}, bf16[4,2,32,128]{3,2,1,0:T(8,128)(2,1)S(1)}, bf16[8,32,128]{2,1,0:T(8,128)(2,1)}, f32[8,1,128]{2...) while((s32[]{:T(128)}, f32[8,32,128]{2,1,0:T(8,128)S(1)}, ...), condition=%wide.region_2.3_spmd.clone, body=%wide.region_1.2_spmd.clone.sunk | while | flops 371433984 | bytes 26279644 | solution.py:65
  7.5 0.9 select_multiply_fusion.2
  8.5 7.6 %all-to-all-start = ((bf16[32,2,32,128]{3,2,1,0:T(8,128)(2,1)}), bf16[32,2,32,128]{3,2,1,0:T(8,128)(2,1)S(1)}, u32[]{:S(2)}, u32[]{:S(2)}) async-start(bf16[32,2,32,128]{3,2,1,0:T(8,128)(2,1)} %select_multiply_fusion.2), calls=%async_computation | async-start | bytes 1048576 | tf_op jit(solution)/shard_map/while/body/eval_jaxpr/all_to_all | solution.py:58
  16.2 29.3 %all_gather.5 = bf16[64,32,128]{2,1,0:T(8,128)(2,1)S(1)} all-gather(bf16[8,32,128]{2,1,0:T(8,128)(2,1)} %get-tuple-element.261), channel_id=1, replica_groups=mesh['area'=32,'pop'=8] {'pop'}, dimensions={0}, use_global_device_ids=true | all-gather | bytes 589824 | tf_op jit(solution)/shard_map/while/body/eval_jaxpr/all_gather | solution.py:39
  45.8 1.0 gather_fusion
  47.4 4.3 fusion.40
  53.2 3.2 fusion.44
  57.9 0.9 select_multiply_fusion.2
  58.8 7.2 %all-to-all-start = ((bf16[32,2,32,128]{3,2,1,0:T(8,128)(2,1)}), bf16[32,2,32,128]{3,2,1,0:T(8,128)(2,1)S(1)}, u32[]{:S(2)}, u32[]{:S(2)}) async-start(bf16[32,2,32,128]{3,2,1,0:T(8,128)(2,1)} %select_multiply_fusion.2), calls=%async_computation | async-start | bytes 1048576 | tf_op jit(solution)/shard_map/while/body/eval_jaxpr/all_to_all | solution.py:58
  66.1 25.6 %all_gather.5 = bf16[64,32,128]{2,1,0:T(8,128)(2,1)S(1)} all-gather(bf16[8,32,128]{2,1,0:T(8,128)(2,1)} %get-tuple-element.261), channel_id=1, replica_groups=mesh['area'=32,'pop'=8] {'pop'}, dimensions={0}, use_global_device_ids=true | all-gather | bytes 589824 | tf_op jit(solution)/shard_map/while/body/eval_jaxpr/all_gather | solution.py:39
  92.1 1.0 gather_fusion
  93.7 4.3 fusion.40
  99.5 3.2 fusion.44
  104.2 0.9 select_multiply_fusion.2
  105.1 7.3 %all-to-all-start = ((bf16[32,2,32,128]{3,2,1,0:T(8,128)(2,1)}), bf16[32,2,32,128]{3,2,1,0:T(8,128)(2,1)S(1)}, u32[]{:S(2)}, u32[]{:S(2)}) async-start(bf16[32,2,32,128]{3,2,1,0:T(8,128)(2,1)} %select_multiply_fusion.2), calls=%async_computation | async-start | bytes 1048576 | tf_op jit(solution)/shard_map/while/body/eval_jaxpr/all_to_all | solution.py:58
  112.5 25.6 %all_gather.5 = bf16[64,32,128]{2,1,0:T(8,128)(2,1)S(1)} all-gather(bf16[8,32,128]{2,1,0:T(8,128)(2,1)} %get-tuple-element.261), channel_id=1, replica_groups=mesh['area'=32,'pop'=8] {'pop'}, dimensions={0}, use_global_device_ids=true | all-gather | bytes 589824 | tf_op jit(solution)/shard_map/while/body/eval_jaxpr/all_gather | solution.py:39
  138.5 1.0 gather_fusion
  140.1 4.3 fusion.40
  145.9 3.2 fusion.44
  150.5 0.9 select_multiply_fusion.2
  151.5 7.3 %all-to-all-start = ((bf16[32,2,32,128]{3,2,1,0:T(8,128)(2,1)}), bf16[32,2,32,128]{3,2,1,0:T(8,128)(2,1)S(1)}, u32[]{:S(2)}, u32[]{:S(2)}) async-start(bf16[32,2,32,128]{3,2,1,0:T(8,128)(2,1)} %select_multiply_fusion.2), calls=%async_computation | async-start | bytes 1048576 | tf_op jit(solution)/shard_map/while/body/eval_jaxpr/all_to_all | solution.py:58
  158.9 25.6 %all_gather.5 = bf16[64,32,128]{2,1,0:T(8,128)(2,1)S(1)} all-gather(bf16[8,32,128]{2,1,0:T(8,128)(2,1)} %get-tuple-element.261), channel_id=1, replica_groups=mesh['area'=32,'pop'=8] {'pop'}, dimensions={0}, use_global_device_ids=true | all-gather | bytes 589824 | tf_op jit(solution)/shard_map/while/body/eval_jaxpr/all_gather | solution.py:39
  184.9 1.0 gather_fusion
  186.5 4.3 fusion.40
  192.3 3.2 fusion.44
  196.9 0.9 select_multiply_fusion.2
  197.9 7.3 %all-to-all-start = ((bf16[32,2,32,128]{3,2,1,0:T(8,128)(2,1)}), bf16[32,2,32,128]{3,2,1,0:T(8,128)(2,1)S(1)}, u32[]{:S(2)}, u32[]{:S(2)}) async-start(bf16[32,2,32,128]{3,2,1,0:T(8,128)(2,1)} %select_multiply_fusion.2), calls=%async_computation | async-start | bytes 1048576 | tf_op jit(solution)/shard_map/while/body/eval_jaxpr/all_to_all | solution.py:58
  205.2 25.6 %all_gather.5 = bf16[64,32,128]{2,1,0:T(8,128)(2,1)S(1)} all-gather(bf16[8,32,128]{2,1,0:T(8,128)(2,1)} %get-tuple-element.261), channel_id=1, replica_groups=mesh['area'=32,'pop'=8] {'pop'}, dimensions={0}, use_global_device_ids=true | all-gather | bytes 589824 | tf_op jit(solution)/shard_map/while/body/eval_jaxpr/all_gather | solution.py:39
  231.3 1.0 gather_fusion
  232.9 4.3 fusion.40
  238.6 3.2 fusion.44
  243.3 0.9 select_multiply_fusion.2
  244.2 7.2 %all-to-all-start = ((bf16[32,2,32,128]{3,2,1,0:T(8,128)(2,1)}), bf16[32,2,32,128]{3,2,1,0:T(8,128)(2,1)S(1)}, u32[]{:S(2)}, u32[]{:S(2)}) async-start(bf16[32,2,32,128]{3,2,1,0:T(8,128)(2,1)} %select_multiply_fusion.2), calls=%async_computation | async-start | bytes 1048576 | tf_op jit(solution)/shard_map/while/body/eval_jaxpr/all_to_all | solution.py:58
  251.6 25.6 %all_gather.5 = bf16[64,32,128]{2,1,0:T(8,128)(2,1)S(1)} all-gather(bf16[8,32,128]{2,1,0:T(8,128)(2,1)} %get-tuple-element.261), channel_id=1, replica_groups=mesh['area'=32,'pop'=8] {'pop'}, dimensions={0}, use_global_device_ids=true | all-gather | bytes 589824 | tf_op jit(solution)/shard_map/while/body/eval_jaxpr/all_gather | solution.py:39
  277.6 1.0 gather_fusion
  279.2 4.3 fusion.40
  285.0 3.2 fusion.44
  289.7 0.9 select_multiply_fusion.2
  290.6 7.2 %all-to-all-start = ((bf16[32,2,32,128]{3,2,1,0:T(8,128)(2,1)}), bf16[32,2,32,128]{3,2,1,0:T(8,128)(2,1)S(1)}, u32[]{:S(2)}, u32[]{:S(2)}) async-start(bf16[32,2,32,128]{3,2,1,0:T(8,128)(2,1)} %select_multiply_fusion.2), calls=%async_computation | async-start | bytes 1048576 | tf_op jit(solution)/shard_map/while/body/eval_jaxpr/all_to_all | solution.py:58
  297.9 25.7 %all_gather.5 = bf16[64,32,128]{2,1,0:T(8,128)(2,1)S(1)} all-gather(bf16[8,32,128]{2,1,0:T(8,128)(2,1)} %get-tuple-element.261), channel_id=1, replica_groups=mesh['area'=32,'pop'=8] {'pop'}, dimensions={0}, use_global_device_ids=true | all-gather | bytes 589824 | tf_op jit(solution)/shard_map/while/body/eval_jaxpr/all_gather | solution.py:39
  324.0 1.0 gather_fusion
  325.6 4.3 fusion.40
  331.3 3.2 fusion.44
  336.0 0.9 select_multiply_fusion.2
  337.0 7.2 %all-to-all-start = ((bf16[32,2,32,128]{3,2,1,0:T(8,128)(2,1)}), bf16[32,2,32,128]{3,2,1,0:T(8,128)(2,1)S(1)}, u32[]{:S(2)}, u32[]{:S(2)}) async-start(bf16[32,2,32,128]{3,2,1,0:T(8,128)(2,1)} %select_multiply_fusion.2), calls=%async_computation | async-start | bytes 1048576 | tf_op jit(solution)/shard_map/while/body/eval_jaxpr/all_to_all | solution.py:58
  344.3 25.7 %all_gather.5 = bf16[64,32,128]{2,1,0:T(8,128)(2,1)S(1)} all-gather(bf16[8,32,128]{2,1,0:T(8,128)(2,1)} %get-tuple-element.261), channel_id=1, replica_groups=mesh['area'=32,'pop'=8] {'pop'}, dimensions={0}, use_global_device_ids=true | all-gather | bytes 589824 | tf_op jit(solution)/shard_map/while/body/eval_jaxpr/all_gather | solution.py:39
  370.3 1.0 gather_fusion
  371.9 4.3 fusion.40
  377.7 3.2 fusion.44
  382.4 0.9 select_multiply_fusion.2
  383.3 7.2 %all-to-all-start = ((bf16[32,2,32,128]{3,2,1,0:T(8,128)(2,1)}), bf16[32,2,32,128]{3,2,1,0:T(8,128)(2,1)S(1)}, u32[]{:S(2)}, u32[]{:S(2)}) async-start(bf16[32,2,32,128]{3,2,1,0:T(8,128)(2,1)} %select_multiply_fusion.2), calls=%async_computation | async-start | bytes 1048576 | tf_op jit(solution)/shard_map/while/body/eval_jaxpr/all_to_all | solution.py:58
  390.6 25.7 %all_gather.5 = bf16[64,32,128]{2,1,0:T(8,128)(2,1)S(1)} all-gather(bf16[8,32,128]{2,1,0:T(8,128)(2,1)} %get-tuple-element.261), channel_id=1, replica_groups=mesh['area'=32,'pop'=8] {'pop'}, dimensions={0}, use_global_device_ids=true | all-gather | bytes 589824 | tf_op jit(solution)/shard_map/while/body/eval_jaxpr/all_gather | solution.py:39
  416.6 1.0 gather_fusion
  418.3 4.3 fusion.40
  424.0 3.2 fusion.44
  428.7 0.9 select_multiply_fusion.2
  429.6 7.2 %all-to-all-start = ((bf16[32,2,32,128]{3,2,1,0:T(8,128)(2,1)}), bf16[32,2,32,128]{3,2,1,0:T(8,128)(2,1)S(1)}, u32[]{:S(2)}, u32[]{:S(2)}) async-start(bf16[32,2,32,128]{3,2,1,0:T(8,128)(2,1)} %select_multiply_fusion.2), calls=%async_computation | async-start | bytes 1048576 | tf_op jit(solution)/shard_map/while/body/eval_jaxpr/all_to_all | solution.py:58
  436.9 25.7 %all_gather.5 = bf16[64,32,128]{2,1,0:T(8,128)(2,1)S(1)} all-gather(bf16[8,32,128]{2,1,0:T(8,128)(2,1)} %get-tuple-element.261), channel_id=1, replica_groups=mesh['area'=32,'pop'=8] {'pop'}, dimensions={0}, use_global_device_ids=true | all-gather | bytes 589824 | tf_op jit(solution)/shard_map/while/body/eval_jaxpr/all_gather | solution.py:39
  463.0 1.0 gather_fusion
  464.6 4.3 fusion.40
  470.3 3.2 fusion.44
  (309 shorter events, 41.6 us)
Async XLA Ops:
  6.8 9.3 %copy-start.1 = (s32[8,32]{1,0:T(8,128)S(1)}, s32[8,32]{1,0:T(8,128)}, u32[]{:S(2)}) copy-start(s32[8,32]{1,0:T(8,128)} %get-tuple-element.279) | copy-start | bytes 3076 | tf_op jit(solution)/shard_map/while
  6.8 39.0 %copy-start.2 = (f32[8,1,128]{2,0,1:T(8,128)S(1)}, f32[8,1,128]{2,0,1:T(8,128)}, u32[]{:S(2)}) copy-start(f32[8,1,128]{2,0,1:T(8,128)} %get-tuple-element.278) | copy-start | bytes 12292 | tf_op jit(solution)/shard_map/while
  8.5 43.3 %all-to-all-start = ((bf16[32,2,32,128]{3,2,1,0:T(8,128)(2,1)}), bf16[32,2,32,128]{3,2,1,0:T(8,128)(2,1)S(1)}, u32[]{:S(2)}, u32[]{:S(2)}) async-start(bf16[32,2,32,128]{3,2,1,0:T(8,128)(2,1)} %select_multiply_fusion.2), calls=%async_computation | async-start | bytes 1048576 | tf_op jit(solution)/shard_map/while/body/eval_jaxpr/all_to_all | solution.py:58
  57.1 8.9 %copy-start.1 = (s32[8,32]{1,0:T(8,128)S(1)}, s32[8,32]{1,0:T(8,128)}, u32[]{:S(2)}) copy-start(s32[8,32]{1,0:T(8,128)} %get-tuple-element.279) | copy-start | bytes 3076 | tf_op jit(solution)/shard_map/while
  57.1 34.9 %copy-start.2 = (f32[8,1,128]{2,0,1:T(8,128)S(1)}, f32[8,1,128]{2,0,1:T(8,128)}, u32[]{:S(2)}) copy-start(f32[8,1,128]{2,0,1:T(8,128)} %get-tuple-element.278) | copy-start | bytes 12292 | tf_op jit(solution)/shard_map/while
  58.8 39.3 %all-to-all-start = ((bf16[32,2,32,128]{3,2,1,0:T(8,128)(2,1)}), bf16[32,2,32,128]{3,2,1,0:T(8,128)(2,1)S(1)}, u32[]{:S(2)}, u32[]{:S(2)}) async-start(bf16[32,2,32,128]{3,2,1,0:T(8,128)(2,1)} %select_multiply_fusion.2), calls=%async_computation | async-start | bytes 1048576 | tf_op jit(solution)/shard_map/while/body/eval_jaxpr/all_to_all | solution.py:58
  103.4 9.0 %copy-start.1 = (s32[8,32]{1,0:T(8,128)S(1)}, s32[8,32]{1,0:T(8,128)}, u32[]{:S(2)}) copy-start(s32[8,32]{1,0:T(8,128)} %get-tuple-element.279) | copy-start | bytes 3076 | tf_op jit(solution)/shard_map/while
  103.5 35.0 %copy-start.2 = (f32[8,1,128]{2,0,1:T(8,128)S(1)}, f32[8,1,128]{2,0,1:T(8,128)}, u32[]{:S(2)}) copy-start(f32[8,1,128]{2,0,1:T(8,128)} %get-tuple-element.278) | copy-start | bytes 12292 | tf_op jit(solution)/shard_map/while
  105.1 39.4 %all-to-all-start = ((bf16[32,2,32,128]{3,2,1,0:T(8,128)(2,1)}), bf16[32,2,32,128]{3,2,1,0:T(8,128)(2,1)S(1)}, u32[]{:S(2)}, u32[]{:S(2)}) async-start(bf16[32,2,32,128]{3,2,1,0:T(8,128)(2,1)} %select_multiply_fusion.2), calls=%async_computation | async-start | bytes 1048576 | tf_op jit(solution)/shard_map/while/body/eval_jaxpr/all_to_all | solution.py:58
  149.8 9.0 %copy-start.1 = (s32[8,32]{1,0:T(8,128)S(1)}, s32[8,32]{1,0:T(8,128)}, u32[]{:S(2)}) copy-start(s32[8,32]{1,0:T(8,128)} %get-tuple-element.279) | copy-start | bytes 3076 | tf_op jit(solution)/shard_map/while
  149.8 35.0 %copy-start.2 = (f32[8,1,128]{2,0,1:T(8,128)S(1)}, f32[8,1,128]{2,0,1:T(8,128)}, u32[]{:S(2)}) copy-start(f32[8,1,128]{2,0,1:T(8,128)} %get-tuple-element.278) | copy-start | bytes 12292 | tf_op jit(solution)/shard_map/while
  151.5 39.4 %all-to-all-start = ((bf16[32,2,32,128]{3,2,1,0:T(8,128)(2,1)}), bf16[32,2,32,128]{3,2,1,0:T(8,128)(2,1)S(1)}, u32[]{:S(2)}, u32[]{:S(2)}) async-start(bf16[32,2,32,128]{3,2,1,0:T(8,128)(2,1)} %select_multiply_fusion.2), calls=%async_computation | async-start | bytes 1048576 | tf_op jit(solution)/shard_map/while/body/eval_jaxpr/all_to_all | solution.py:58
  196.2 8.9 %copy-start.1 = (s32[8,32]{1,0:T(8,128)S(1)}, s32[8,32]{1,0:T(8,128)}, u32[]{:S(2)}) copy-start(s32[8,32]{1,0:T(8,128)} %get-tuple-element.279) | copy-start | bytes 3076 | tf_op jit(solution)/shard_map/while
  196.2 35.0 %copy-start.2 = (f32[8,1,128]{2,0,1:T(8,128)S(1)}, f32[8,1,128]{2,0,1:T(8,128)}, u32[]{:S(2)}) copy-start(f32[8,1,128]{2,0,1:T(8,128)} %get-tuple-element.278) | copy-start | bytes 12292 | tf_op jit(solution)/shard_map/while
  197.9 39.3 %all-to-all-start = ((bf16[32,2,32,128]{3,2,1,0:T(8,128)(2,1)}), bf16[32,2,32,128]{3,2,1,0:T(8,128)(2,1)S(1)}, u32[]{:S(2)}, u32[]{:S(2)}) async-start(bf16[32,2,32,128]{3,2,1,0:T(8,128)(2,1)} %select_multiply_fusion.2), calls=%async_computation | async-start | bytes 1048576 | tf_op jit(solution)/shard_map/while/body/eval_jaxpr/all_to_all | solution.py:58
  242.6 8.9 %copy-start.1 = (s32[8,32]{1,0:T(8,128)S(1)}, s32[8,32]{1,0:T(8,128)}, u32[]{:S(2)}) copy-start(s32[8,32]{1,0:T(8,128)} %get-tuple-element.279) | copy-start | bytes 3076 | tf_op jit(solution)/shard_map/while
  242.6 35.0 %copy-start.2 = (f32[8,1,128]{2,0,1:T(8,128)S(1)}, f32[8,1,128]{2,0,1:T(8,128)}, u32[]{:S(2)}) copy-start(f32[8,1,128]{2,0,1:T(8,128)} %get-tuple-element.278) | copy-start | bytes 12292 | tf_op jit(solution)/shard_map/while
  244.2 39.3 %all-to-all-start = ((bf16[32,2,32,128]{3,2,1,0:T(8,128)(2,1)}), bf16[32,2,32,128]{3,2,1,0:T(8,128)(2,1)S(1)}, u32[]{:S(2)}, u32[]{:S(2)}) async-start(bf16[32,2,32,128]{3,2,1,0:T(8,128)(2,1)} %select_multiply_fusion.2), calls=%async_computation | async-start | bytes 1048576 | tf_op jit(solution)/shard_map/while/body/eval_jaxpr/all_to_all | solution.py:58
  289.0 8.9 %copy-start.1 = (s32[8,32]{1,0:T(8,128)S(1)}, s32[8,32]{1,0:T(8,128)}, u32[]{:S(2)}) copy-start(s32[8,32]{1,0:T(8,128)} %get-tuple-element.279) | copy-start | bytes 3076 | tf_op jit(solution)/shard_map/while
  289.0 35.0 %copy-start.2 = (f32[8,1,128]{2,0,1:T(8,128)S(1)}, f32[8,1,128]{2,0,1:T(8,128)}, u32[]{:S(2)}) copy-start(f32[8,1,128]{2,0,1:T(8,128)} %get-tuple-element.278) | copy-start | bytes 12292 | tf_op jit(solution)/shard_map/while
  290.6 39.3 %all-to-all-start = ((bf16[32,2,32,128]{3,2,1,0:T(8,128)(2,1)}), bf16[32,2,32,128]{3,2,1,0:T(8,128)(2,1)S(1)}, u32[]{:S(2)}, u32[]{:S(2)}) async-start(bf16[32,2,32,128]{3,2,1,0:T(8,128)(2,1)} %select_multiply_fusion.2), calls=%async_computation | async-start | bytes 1048576 | tf_op jit(solution)/shard_map/while/body/eval_jaxpr/all_to_all | solution.py:58
  335.3 8.9 %copy-start.1 = (s32[8,32]{1,0:T(8,128)S(1)}, s32[8,32]{1,0:T(8,128)}, u32[]{:S(2)}) copy-start(s32[8,32]{1,0:T(8,128)} %get-tuple-element.279) | copy-start | bytes 3076 | tf_op jit(solution)/shard_map/while
  335.3 35.0 %copy-start.2 = (f32[8,1,128]{2,0,1:T(8,128)S(1)}, f32[8,1,128]{2,0,1:T(8,128)}, u32[]{:S(2)}) copy-start(f32[8,1,128]{2,0,1:T(8,128)} %get-tuple-element.278) | copy-start | bytes 12292 | tf_op jit(solution)/shard_map/while
  337.0 39.3 %all-to-all-start = ((bf16[32,2,32,128]{3,2,1,0:T(8,128)(2,1)}), bf16[32,2,32,128]{3,2,1,0:T(8,128)(2,1)S(1)}, u32[]{:S(2)}, u32[]{:S(2)}) async-start(bf16[32,2,32,128]{3,2,1,0:T(8,128)(2,1)} %select_multiply_fusion.2), calls=%async_computation | async-start | bytes 1048576 | tf_op jit(solution)/shard_map/while/body/eval_jaxpr/all_to_all | solution.py:58
  381.6 8.9 %copy-start.1 = (s32[8,32]{1,0:T(8,128)S(1)}, s32[8,32]{1,0:T(8,128)}, u32[]{:S(2)}) copy-start(s32[8,32]{1,0:T(8,128)} %get-tuple-element.279) | copy-start | bytes 3076 | tf_op jit(solution)/shard_map/while
  381.6 35.0 %copy-start.2 = (f32[8,1,128]{2,0,1:T(8,128)S(1)}, f32[8,1,128]{2,0,1:T(8,128)}, u32[]{:S(2)}) copy-start(f32[8,1,128]{2,0,1:T(8,128)} %get-tuple-element.278) | copy-start | bytes 12292 | tf_op jit(solution)/shard_map/while
  383.3 39.3 %all-to-all-start = ((bf16[32,2,32,128]{3,2,1,0:T(8,128)(2,1)}), bf16[32,2,32,128]{3,2,1,0:T(8,128)(2,1)S(1)}, u32[]{:S(2)}, u32[]{:S(2)}) async-start(bf16[32,2,32,128]{3,2,1,0:T(8,128)(2,1)} %select_multiply_fusion.2), calls=%async_computation | async-start | bytes 1048576 | tf_op jit(solution)/shard_map/while/body/eval_jaxpr/all_to_all | solution.py:58
  428.0 8.9 %copy-start.1 = (s32[8,32]{1,0:T(8,128)S(1)}, s32[8,32]{1,0:T(8,128)}, u32[]{:S(2)}) copy-start(s32[8,32]{1,0:T(8,128)} %get-tuple-element.279) | copy-start | bytes 3076 | tf_op jit(solution)/shard_map/while
  428.0 35.0 %copy-start.2 = (f32[8,1,128]{2,0,1:T(8,128)S(1)}, f32[8,1,128]{2,0,1:T(8,128)}, u32[]{:S(2)}) copy-start(f32[8,1,128]{2,0,1:T(8,128)} %get-tuple-element.278) | copy-start | bytes 12292 | tf_op jit(solution)/shard_map/while
  429.6 39.3 %all-to-all-start = ((bf16[32,2,32,128]{3,2,1,0:T(8,128)(2,1)}), bf16[32,2,32,128]{3,2,1,0:T(8,128)(2,1)S(1)}, u32[]{:S(2)}, u32[]{:S(2)}) async-start(bf16[32,2,32,128]{3,2,1,0:T(8,128)(2,1)} %select_multiply_fusion.2), calls=%async_computation | async-start | bytes 1048576 | tf_op jit(solution)/shard_map/while/body/eval_jaxpr/all_to_all | solution.py:58
  474.3 0.7 copy-start
where the time goes:
time: 478 us; the launch traced here: 475 us
  blocking collectives  260 us (54%)
  matrix products  75.3 us (16%)
  starting transfers between devices  72.8 us (15%)
  local copies, waits for them, and re-layouts  42.8 us (9%)
  other arithmetic  21.9 us (5%)
    all_gather x10, blocking collectives, advance(): area_rates = lax.all_gather(rate_now, 'pop', axis=0, tiled=True)  260 us
    all_to_all x10, starting transfers between devices, turn_slots(): lax.all_to_all(chosen, 'area', split_axis=0, concat_axis=0, tiled=True)  72.8 us
    dot_general x10, matrix products, advance(): jnp.einsum('rkji,rktj->rti', w_inner, tile_rows, preferred_element_type=j...  43.2 us
    dot_general x10, matrix products, advance(): jnp.einsum('rkji,rktj->rti', w_outer, source_rows, preferred_element_type...  32.1 us
    gather x10, local copies, waits for them, and re-layouts, advance(): tile_rows = jnp.take(area_rates, tile_index, axis=0)  9.94 us
  transfers between devices with their start and end apart: 10, of which 0 were waited for; matrix products, arithmetic and copies ran while one was open for 13% of the time, Pallas kernels for 0%

commit v1 on v0

--- a/solution.py
+++ b/solution.py
@@ -36,7 +36,10 @@
     drive_ext = external[0].astype(jnp.float32)
 
     def advance(activity, rate_now, edge_rows):
-        area_rates = lax.all_gather(rate_now, "pop", axis=0, tiled=True)
+        size = lax.axis_size("pop")
+        pieces = jnp.stack([rate_now for _ in range(size)])
+        pieces = lax.all_to_all(pieces, "pop", split_axis=0, concat_axis=0)
+        area_rates = jnp.concatenate(pieces, axis=0)
         tile_rows = jnp.take(area_rates, tile_index, axis=0)
         inner_term = jnp.einsum(
             "rkji,rktj->rti", w_inner, tile_rows, preferred_element_type=jnp.float32

time: 478 us -> 483 us (1.010)
  blocking collectives: 260 us -> 0 us
  waiting for transfers between devices: 0.03 us -> 247 us
  starting transfers between devices: 72.8 us -> 104 us
  matrix products: 75.3 us -> 51.3 us
  local copies, waits for them, and re-layouts: 42.8 us -> 50.1 us
    all_gather x10 -> x0, blocking collectives: 260 us -> none  [advance(): area_rates = lax.all_gather(rate_now, 'pop', axis=0, tiled=True)]
    all_to_all x0 -> x10, waiting for transfers between devices: none -> 152 us  [advance(): pieces = lax.all_to_all(pieces, 'pop', split_axis=0, concat_axis=0)]
    all_to_all x10, waiting for transfers between devices: 0.03 us -> 95.1 us  [turn_slots(): lax.all_to_all(chosen, 'area', split_axis=0, concat_axis=0, tiled=True)]
    all_to_all x0 -> x10, starting transfers between devices: none -> 39.9 us  [advance(): pieces = lax.all_to_all(pieces, 'pop', split_axis=0, concat_axis=0)]
    dot_general x10, matrix products: 32.1 us -> 6.86 us  [advance(): jnp.einsum('rkji,rktj->rti', w_outer, source_rows, preferred_element_type...]
    another operation x0 -> x10, local copies, waits for them, and re-layouts: none -> 8.75 us  [advance(): pieces = jnp.stack([rate_now for _ in range(size)])]
    all_to_all x10, starting transfers between devices: 72.8 us -> 64.2 us  [turn_slots(): lax.all_to_all(chosen, 'area', split_axis=0, concat_axis=0, tiled=True)]
    broadcast_in_dim x10, local copies, waits for them, and re-layouts: 7.18 us -> 0.03 us  [turn_slots(): sent_hist = jnp.concatenate([rate_now[None, :SEND_DEV], sent_hist[:-1]], 0)]
  transfers between devices with their start and end apart: 10 -> 20, of which waited for: 0 -> 20; matrix products, arithmetic and copies ran while one was open for 13% -> 5% of each run, Pallas kernels for 0% -> 0%
where the time goes in v1:
time: 483 us; the launch traced here: 477 us
  waiting for transfers between devices  247 us (51%)
  starting transfers between devices  104 us (22%)
  matrix products  51.3 us (11%)
  local copies, waits for them, and re-layouts  50.1 us (10%)
  other arithmetic  22.1 us (5%)
    all_to_all x10, waiting for transfers between devices, advance(): pieces = lax.all_to_all(pieces, 'pop', split_axis=0, concat_axis=0)  152 us
    all_to_all x10, waiting for transfers between devices, turn_slots(): lax.all_to_all(chosen, 'area', split_axis=0, concat_axis=0, tiled=True)  95.1 us
    all_to_all x10, starting transfers between devices, turn_slots(): lax.all_to_all(chosen, 'area', split_axis=0, concat_axis=0, tiled=True)  64.2 us
    dot_general x10, matrix products, advance(): jnp.einsum('rkji,rktj->rti', w_inner, tile_rows, preferred_element_type=j...  44.5 us
    all_to_all x10, starting transfers between devices, advance(): pieces = lax.all_to_all(pieces, 'pop', split_axis=0, concat_axis=0)  39.9 us
    gather x10, local copies, waits for them, and re-layouts, advance(): tile_rows = jnp.take(area_rates, tile_index, axis=0)  9.93 us
  transfers between devices with their start and end apart: 20, of which 20 were waited for; matrix products, arithmetic and copies ran while one was open for 5% of the time, Pallas kernels for 0%

profile of v1, /device:TPU:4, one launch (start us, length us, event | category | flops | bytes accessed | tf_op | source)
XLA Modules:
  0.0 477.4 jit_solution(3095026721901738118)
XLA Ops:
  0.0 1.3 dynamic_slice.6
  1.9 1.1 fusion.23
  3.0 1.6 slice_bitcast_fusion.1
  6.9 470.4 %while.15 = (s32[]{:T(128)}, f32[8,32,128]{2,1,0:T(8,128)}, bf16[4,2,32,128]{3,2,1,0:T(8,128)(2,1)S(1)}, bf16[8,32,128]{2,1,0:T(8,128)(2,1)S(1)}, f32[8,1,128]{2...) while((s32[]{:T(128)}, f32[8,32,128]{2,1,0:T(8,128)}, ...), condition=%wide.region_2.3_spmd.clone, body=%wide.region_1.2_spmd.clone.sunk | while | flops 371433984 | bytes 42008428 | solution.py:68
  8.6 7.6 %all-to-all-start.1 = ((bf16[32,2,32,128]{3,2,1,0:T(8,128)(2,1)}), bf16[32,2,32,128]{3,2,1,0:T(8,128)(2,1)S(1)}, u32[]{:S(2)}, u32[]{:S(2)}) async-start(bf16[32,2,32,128]{3,2,1,0:T(8,128)(2,1)} %select_multiply_fusion.2), calls=%async_computation.1 | async-start | bytes 1048576 | tf_op jit(solution)/shard_map/while/body/eval_jaxpr/all_to_all | solution.py:61
  16.4 9.4 %all-to-all-done.1 = bf16[32,2,32,128]{3,2,1,0:T(8,128)(2,1)S(1)} async-done(((bf16[32,2,32,128]{3,2,1,0:T(8,128)(2,1)}), bf16[32,2,32,128]{3,2,1,0:T(8,128)(2,1)S(1)}, u32[]{:S(2)}, u32[]{:S(2)}) %all-to-all-start.1) | async-done | bytes 524320 | tf_op jit(solution)/shard_map/while/body/eval_jaxpr/all_to_all | solution.py:61
  26.7 8.5 %all-to-all-start = ((bf16[8,8,32,128]{3,2,1,0:T(8,128)(2,1)}), bf16[8,8,32,128]{3,2,1,0:T(8,128)(2,1)S(1)}, u32[]{:S(2)}, u32[]{:S(2)}) async-start(bf16[8,8,32,128]{3,2,1,0:T(8,128)(2,1)} %stack.4), calls=%async_computation | async-start | bytes 1048576 | tf_op jit(solution)/shard_map/while/body/eval_jaxpr/all_to_all | solution.py:41
  37.5 15.0 %all-to-all-done = bf16[8,8,32,128]{3,2,1,0:T(8,128)(2,1)S(1)} async-done(((bf16[8,8,32,128]{3,2,1,0:T(8,128)(2,1)}), bf16[8,8,32,128]{3,2,1,0:T(8,128)(2,1)S(1)}, u32[]{:S(2)}, u32[]{:S(2)}) %all-to-all-start) | async-done | bytes 524320 | tf_op jit(solution)/shard_map/while/body/eval_jaxpr/all_to_all | solution.py:41
  52.5 1.0 gather_fusion
  53.5 4.4 fusion.40
  61.0 6.4 %all-to-all-start.1 = ((bf16[32,2,32,128]{3,2,1,0:T(8,128)(2,1)}), bf16[32,2,32,128]{3,2,1,0:T(8,128)(2,1)S(1)}, u32[]{:S(2)}, u32[]{:S(2)}) async-start(bf16[32,2,32,128]{3,2,1,0:T(8,128)(2,1)} %select_multiply_fusion.2), calls=%async_computation.1 | async-start | bytes 1048576 | tf_op jit(solution)/shard_map/while/body/eval_jaxpr/all_to_all | solution.py:61
  67.6 9.4 %all-to-all-done.1 = bf16[32,2,32,128]{3,2,1,0:T(8,128)(2,1)S(1)} async-done(((bf16[32,2,32,128]{3,2,1,0:T(8,128)(2,1)}), bf16[32,2,32,128]{3,2,1,0:T(8,128)(2,1)S(1)}, u32[]{:S(2)}, u32[]{:S(2)}) %all-to-all-start.1) | async-done | bytes 524320 | tf_op jit(solution)/shard_map/while/body/eval_jaxpr/all_to_all | solution.py:61
  77.9 3.5 all-to-all-start
  83.7 15.2 %all-to-all-done = bf16[8,8,32,128]{3,2,1,0:T(8,128)(2,1)S(1)} async-done(((bf16[8,8,32,128]{3,2,1,0:T(8,128)(2,1)}), bf16[8,8,32,128]{3,2,1,0:T(8,128)(2,1)S(1)}, u32[]{:S(2)}, u32[]{:S(2)}) %all-to-all-start) | async-done | bytes 524320 | tf_op jit(solution)/shard_map/while/body/eval_jaxpr/all_to_all | solution.py:41
  99.0 1.0 gather_fusion
  100.0 4.4 fusion.40
  107.4 6.3 %all-to-all-start.1 = ((bf16[32,2,32,128]{3,2,1,0:T(8,128)(2,1)}), bf16[32,2,32,128]{3,2,1,0:T(8,128)(2,1)S(1)}, u32[]{:S(2)}, u32[]{:S(2)}) async-start(bf16[32,2,32,128]{3,2,1,0:T(8,128)(2,1)} %select_multiply_fusion.2), calls=%async_computation.1 | async-start | bytes 1048576 | tf_op jit(solution)/shard_map/while/body/eval_jaxpr/all_to_all | solution.py:61
  114.0 9.5 %all-to-all-done.1 = bf16[32,2,32,128]{3,2,1,0:T(8,128)(2,1)S(1)} async-done(((bf16[32,2,32,128]{3,2,1,0:T(8,128)(2,1)}), bf16[32,2,32,128]{3,2,1,0:T(8,128)(2,1)S(1)}, u32[]{:S(2)}, u32[]{:S(2)}) %all-to-all-start.1) | async-done | bytes 524320 | tf_op jit(solution)/shard_map/while/body/eval_jaxpr/all_to_all | solution.py:61
  124.4 3.5 all-to-all-start
  130.2 15.2 %all-to-all-done = bf16[8,8,32,128]{3,2,1,0:T(8,128)(2,1)S(1)} async-done(((bf16[8,8,32,128]{3,2,1,0:T(8,128)(2,1)}), bf16[8,8,32,128]{3,2,1,0:T(8,128)(2,1)S(1)}, u32[]{:S(2)}, u32[]{:S(2)}) %all-to-all-start) | async-done | bytes 524320 | tf_op jit(solution)/shard_map/while/body/eval_jaxpr/all_to_all | solution.py:41
  145.4 1.0 gather_fusion
  146.4 4.4 fusion.40
  153.9 6.3 %all-to-all-start.1 = ((bf16[32,2,32,128]{3,2,1,0:T(8,128)(2,1)}), bf16[32,2,32,128]{3,2,1,0:T(8,128)(2,1)S(1)}, u32[]{:S(2)}, u32[]{:S(2)}) async-start(bf16[32,2,32,128]{3,2,1,0:T(8,128)(2,1)} %select_multiply_fusion.2), calls=%async_computation.1 | async-start | bytes 1048576 | tf_op jit(solution)/shard_map/while/body/eval_jaxpr/all_to_all | solution.py:61
  160.4 9.5 %all-to-all-done.1 = bf16[32,2,32,128]{3,2,1,0:T(8,128)(2,1)S(1)} async-done(((bf16[32,2,32,128]{3,2,1,0:T(8,128)(2,1)}), bf16[32,2,32,128]{3,2,1,0:T(8,128)(2,1)S(1)}, u32[]{:S(2)}, u32[]{:S(2)}) %all-to-all-start.1) | async-done | bytes 524320 | tf_op jit(solution)/shard_map/while/body/eval_jaxpr/all_to_all | solution.py:61
  170.8 3.5 all-to-all-start
  176.6 15.2 %all-to-all-done = bf16[8,8,32,128]{3,2,1,0:T(8,128)(2,1)S(1)} async-done(((bf16[8,8,32,128]{3,2,1,0:T(8,128)(2,1)}), bf16[8,8,32,128]{3,2,1,0:T(8,128)(2,1)S(1)}, u32[]{:S(2)}, u32[]{:S(2)}) %all-to-all-start) | async-done | bytes 524320 | tf_op jit(solution)/shard_map/while/body/eval_jaxpr/all_to_all | solution.py:41
  191.8 1.0 gather_fusion
  192.9 4.4 fusion.40
  200.3 6.3 %all-to-all-start.1 = ((bf16[32,2,32,128]{3,2,1,0:T(8,128)(2,1)}), bf16[32,2,32,128]{3,2,1,0:T(8,128)(2,1)S(1)}, u32[]{:S(2)}, u32[]{:S(2)}) async-start(bf16[32,2,32,128]{3,2,1,0:T(8,128)(2,1)} %select_multiply_fusion.2), calls=%async_computation.1 | async-start | bytes 1048576 | tf_op jit(solution)/shard_map/while/body/eval_jaxpr/all_to_all | solution.py:61
  206.9 9.5 %all-to-all-done.1 = bf16[32,2,32,128]{3,2,1,0:T(8,128)(2,1)S(1)} async-done(((bf16[32,2,32,128]{3,2,1,0:T(8,128)(2,1)}), bf16[32,2,32,128]{3,2,1,0:T(8,128)(2,1)S(1)}, u32[]{:S(2)}, u32[]{:S(2)}) %all-to-all-start.1) | async-done | bytes 524320 | tf_op jit(solution)/shard_map/while/body/eval_jaxpr/all_to_all | solution.py:61
  217.3 3.5 all-to-all-start
  223.0 15.2 %all-to-all-done = bf16[8,8,32,128]{3,2,1,0:T(8,128)(2,1)S(1)} async-done(((bf16[8,8,32,128]{3,2,1,0:T(8,128)(2,1)}), bf16[8,8,32,128]{3,2,1,0:T(8,128)(2,1)S(1)}, u32[]{:S(2)}, u32[]{:S(2)}) %all-to-all-start) | async-done | bytes 524320 | tf_op jit(solution)/shard_map/while/body/eval_jaxpr/all_to_all | solution.py:41
  238.3 1.0 gather_fusion
  239.3 4.4 fusion.40
  246.8 6.3 %all-to-all-start.1 = ((bf16[32,2,32,128]{3,2,1,0:T(8,128)(2,1)}), bf16[32,2,32,128]{3,2,1,0:T(8,128)(2,1)S(1)}, u32[]{:S(2)}, u32[]{:S(2)}) async-start(bf16[32,2,32,128]{3,2,1,0:T(8,128)(2,1)} %select_multiply_fusion.2), calls=%async_computation.1 | async-start | bytes 1048576 | tf_op jit(solution)/shard_map/while/body/eval_jaxpr/all_to_all | solution.py:61
  253.3 9.5 %all-to-all-done.1 = bf16[32,2,32,128]{3,2,1,0:T(8,128)(2,1)S(1)} async-done(((bf16[32,2,32,128]{3,2,1,0:T(8,128)(2,1)}), bf16[32,2,32,128]{3,2,1,0:T(8,128)(2,1)S(1)}, u32[]{:S(2)}, u32[]{:S(2)}) %all-to-all-start.1) | async-done | bytes 524320 | tf_op jit(solution)/shard_map/while/body/eval_jaxpr/all_to_all | solution.py:61
  263.7 3.5 all-to-all-start
  269.5 15.2 %all-to-all-done = bf16[8,8,32,128]{3,2,1,0:T(8,128)(2,1)S(1)} async-done(((bf16[8,8,32,128]{3,2,1,0:T(8,128)(2,1)}), bf16[8,8,32,128]{3,2,1,0:T(8,128)(2,1)S(1)}, u32[]{:S(2)}, u32[]{:S(2)}) %all-to-all-start) | async-done | bytes 524320 | tf_op jit(solution)/shard_map/while/body/eval_jaxpr/all_to_all | solution.py:41
  284.7 1.0 gather_fusion
  285.7 4.4 fusion.40
  293.2 6.3 %all-to-all-start.1 = ((bf16[32,2,32,128]{3,2,1,0:T(8,128)(2,1)}), bf16[32,2,32,128]{3,2,1,0:T(8,128)(2,1)S(1)}, u32[]{:S(2)}, u32[]{:S(2)}) async-start(bf16[32,2,32,128]{3,2,1,0:T(8,128)(2,1)} %select_multiply_fusion.2), calls=%async_computation.1 | async-start | bytes 1048576 | tf_op jit(solution)/shard_map/while/body/eval_jaxpr/all_to_all | solution.py:61
  299.7 9.5 %all-to-all-done.1 = bf16[32,2,32,128]{3,2,1,0:T(8,128)(2,1)S(1)} async-done(((bf16[32,2,32,128]{3,2,1,0:T(8,128)(2,1)}), bf16[32,2,32,128]{3,2,1,0:T(8,128)(2,1)S(1)}, u32[]{:S(2)}, u32[]{:S(2)}) %all-to-all-start.1) | async-done | bytes 524320 | tf_op jit(solution)/shard_map/while/body/eval_jaxpr/all_to_all | solution.py:61
  310.1 3.5 all-to-all-start
  315.9 15.2 %all-to-all-done = bf16[8,8,32,128]{3,2,1,0:T(8,128)(2,1)S(1)} async-done(((bf16[8,8,32,128]{3,2,1,0:T(8,128)(2,1)}), bf16[8,8,32,128]{3,2,1,0:T(8,128)(2,1)S(1)}, u32[]{:S(2)}, u32[]{:S(2)}) %all-to-all-start) | async-done | bytes 524320 | tf_op jit(solution)/shard_map/while/body/eval_jaxpr/all_to_all | solution.py:41
  331.2 1.0 gather_fusion
  332.2 4.4 fusion.40
  339.7 6.3 %all-to-all-start.1 = ((bf16[32,2,32,128]{3,2,1,0:T(8,128)(2,1)}), bf16[32,2,32,128]{3,2,1,0:T(8,128)(2,1)S(1)}, u32[]{:S(2)}, u32[]{:S(2)}) async-start(bf16[32,2,32,128]{3,2,1,0:T(8,128)(2,1)} %select_multiply_fusion.2), calls=%async_computation.1 | async-start | bytes 1048576 | tf_op jit(solution)/shard_map/while/body/eval_jaxpr/all_to_all | solution.py:61
  346.2 9.5 %all-to-all-done.1 = bf16[32,2,32,128]{3,2,1,0:T(8,128)(2,1)S(1)} async-done(((bf16[32,2,32,128]{3,2,1,0:T(8,128)(2,1)}), bf16[32,2,32,128]{3,2,1,0:T(8,128)(2,1)S(1)}, u32[]{:S(2)}, u32[]{:S(2)}) %all-to-all-start.1) | async-done | bytes 524320 | tf_op jit(solution)/shard_map/while/body/eval_jaxpr/all_to_all | solution.py:61
  356.6 3.5 all-to-all-start
  362.4 15.2 %all-to-all-done = bf16[8,8,32,128]{3,2,1,0:T(8,128)(2,1)S(1)} async-done(((bf16[8,8,32,128]{3,2,1,0:T(8,128)(2,1)}), bf16[8,8,32,128]{3,2,1,0:T(8,128)(2,1)S(1)}, u32[]{:S(2)}, u32[]{:S(2)}) %all-to-all-start) | async-done | bytes 524320 | tf_op jit(solution)/shard_map/while/body/eval_jaxpr/all_to_all | solution.py:41
  377.6 1.0 gather_fusion
  378.6 4.4 fusion.40
  386.1 6.3 %all-to-all-start.1 = ((bf16[32,2,32,128]{3,2,1,0:T(8,128)(2,1)}), bf16[32,2,32,128]{3,2,1,0:T(8,128)(2,1)S(1)}, u32[]{:S(2)}, u32[]{:S(2)}) async-start(bf16[32,2,32,128]{3,2,1,0:T(8,128)(2,1)} %select_multiply_fusion.2), calls=%async_computation.1 | async-start | bytes 1048576 | tf_op jit(solution)/shard_map/while/body/eval_jaxpr/all_to_all | solution.py:61
  392.6 9.5 %all-to-all-done.1 = bf16[32,2,32,128]{3,2,1,0:T(8,128)(2,1)S(1)} async-done(((bf16[32,2,32,128]{3,2,1,0:T(8,128)(2,1)}), bf16[32,2,32,128]{3,2,1,0:T(8,128)(2,1)S(1)}, u32[]{:S(2)}, u32[]{:S(2)}) %all-to-all-start.1) | async-done | bytes 524320 | tf_op jit(solution)/shard_map/while/body/eval_jaxpr/all_to_all | solution.py:61
  403.0 3.5 all-to-all-start
  408.8 15.2 %all-to-all-done = bf16[8,8,32,128]{3,2,1,0:T(8,128)(2,1)S(1)} async-done(((bf16[8,8,32,128]{3,2,1,0:T(8,128)(2,1)}), bf16[8,8,32,128]{3,2,1,0:T(8,128)(2,1)S(1)}, u32[]{:S(2)}, u32[]{:S(2)}) %all-to-all-start) | async-done | bytes 524320 | tf_op jit(solution)/shard_map/while/body/eval_jaxpr/all_to_all | solution.py:41
  424.0 1.0 gather_fusion
  425.1 4.4 fusion.40
  432.5 6.3 %all-to-all-start.1 = ((bf16[32,2,32,128]{3,2,1,0:T(8,128)(2,1)}), bf16[32,2,32,128]{3,2,1,0:T(8,128)(2,1)S(1)}, u32[]{:S(2)}, u32[]{:S(2)}) async-start(bf16[32,2,32,128]{3,2,1,0:T(8,128)(2,1)} %select_multiply_fusion.2), calls=%async_computation.1 | async-start | bytes 1048576 | tf_op jit(solution)/shard_map/while/body/eval_jaxpr/all_to_all | solution.py:61
  439.1 9.5 %all-to-all-done.1 = bf16[32,2,32,128]{3,2,1,0:T(8,128)(2,1)S(1)} async-done(((bf16[32,2,32,128]{3,2,1,0:T(8,128)(2,1)}), bf16[32,2,32,128]{3,2,1,0:T(8,128)(2,1)S(1)}, u32[]{:S(2)}, u32[]{:S(2)}) %all-to-all-start.1) | async-done | bytes 524320 | tf_op jit(solution)/shard_map/while/body/eval_jaxpr/all_to_all | solution.py:61
  449.5 3.5 all-to-all-start
  455.3 15.2 %all-to-all-done = bf16[8,8,32,128]{3,2,1,0:T(8,128)(2,1)S(1)} async-done(((bf16[8,8,32,128]{3,2,1,0:T(8,128)(2,1)}), bf16[8,8,32,128]{3,2,1,0:T(8,128)(2,1)S(1)}, u32[]{:S(2)}, u32[]{:S(2)}) %all-to-all-start) | async-done | bytes 524320 | tf_op jit(solution)/shard_map/while/body/eval_jaxpr/all_to_all | solution.py:41
  470.5 1.0 gather_fusion
  471.5 4.4 fusion.40
  (407 shorter events, 65.2 us)
Async XLA Ops:
  6.9 9.3 %copy-start.4 = (s32[8,32]{1,0:T(8,128)S(1)}, s32[8,32]{1,0:T(8,128)}, u32[]{:S(2)}) copy-start(s32[8,32]{1,0:T(8,128)} %get-tuple-element.279) | copy-start | bytes 3076 | tf_op jit(solution)/shard_map/while
  7.6 28.4 %copy-start.5 = (f32[8,1,128]{2,0,1:T(8,128)S(1)}, f32[8,1,128]{2,0,1:T(8,128)}, u32[]{:S(2)}) copy-start(f32[8,1,128]{2,0,1:T(8,128)} %get-tuple-element.278) | copy-start | bytes 12292 | tf_op jit(solution)/shard_map/while
  8.6 17.3 %all-to-all-start.1 = ((bf16[32,2,32,128]{3,2,1,0:T(8,128)(2,1)}), bf16[32,2,32,128]{3,2,1,0:T(8,128)(2,1)S(1)}, u32[]{:S(2)}, u32[]{:S(2)}) async-start(bf16[32,2,32,128]{3,2,1,0:T(8,128)(2,1)} %select_multiply_fusion.2), calls=%async_computation.1 | async-start | bytes 1048576 | tf_op jit(solution)/shard_map/while/body/eval_jaxpr/all_to_all | solution.py:61
  26.7 25.8 %all-to-all-start = ((bf16[8,8,32,128]{3,2,1,0:T(8,128)(2,1)}), bf16[8,8,32,128]{3,2,1,0:T(8,128)(2,1)S(1)}, u32[]{:S(2)}, u32[]{:S(2)}) async-start(bf16[8,8,32,128]{3,2,1,0:T(8,128)(2,1)} %stack.4), calls=%async_computation | async-start | bytes 1048576 | tf_op jit(solution)/shard_map/while/body/eval_jaxpr/all_to_all | solution.py:41
  53.5 4.5 copy-start
  59.4 8.0 %copy-start.4 = (s32[8,32]{1,0:T(8,128)S(1)}, s32[8,32]{1,0:T(8,128)}, u32[]{:S(2)}) copy-start(s32[8,32]{1,0:T(8,128)} %get-tuple-element.279) | copy-start | bytes 3076 | tf_op jit(solution)/shard_map/while
  60.1 22.2 %copy-start.5 = (f32[8,1,128]{2,0,1:T(8,128)S(1)}, f32[8,1,128]{2,0,1:T(8,128)}, u32[]{:S(2)}) copy-start(f32[8,1,128]{2,0,1:T(8,128)} %get-tuple-element.278) | copy-start | bytes 12292 | tf_op jit(solution)/shard_map/while
  61.0 16.1 %all-to-all-start.1 = ((bf16[32,2,32,128]{3,2,1,0:T(8,128)(2,1)}), bf16[32,2,32,128]{3,2,1,0:T(8,128)(2,1)S(1)}, u32[]{:S(2)}, u32[]{:S(2)}) async-start(bf16[32,2,32,128]{3,2,1,0:T(8,128)(2,1)} %select_multiply_fusion.2), calls=%async_computation.1 | async-start | bytes 1048576 | tf_op jit(solution)/shard_map/while/body/eval_jaxpr/all_to_all | solution.py:61
  77.9 21.0 %all-to-all-start = ((bf16[8,8,32,128]{3,2,1,0:T(8,128)(2,1)}), bf16[8,8,32,128]{3,2,1,0:T(8,128)(2,1)S(1)}, u32[]{:S(2)}, u32[]{:S(2)}) async-start(bf16[8,8,32,128]{3,2,1,0:T(8,128)(2,1)} %stack.4), calls=%async_computation | async-start | bytes 1048576 | tf_op jit(solution)/shard_map/while/body/eval_jaxpr/all_to_all | solution.py:41
  100.0 4.5 copy-start
  105.8 7.9 %copy-start.4 = (s32[8,32]{1,0:T(8,128)S(1)}, s32[8,32]{1,0:T(8,128)}, u32[]{:S(2)}) copy-start(s32[8,32]{1,0:T(8,128)} %get-tuple-element.279) | copy-start | bytes 3076 | tf_op jit(solution)/shard_map/while
  106.5 22.2 %copy-start.5 = (f32[8,1,128]{2,0,1:T(8,128)S(1)}, f32[8,1,128]{2,0,1:T(8,128)}, u32[]{:S(2)}) copy-start(f32[8,1,128]{2,0,1:T(8,128)} %get-tuple-element.278) | copy-start | bytes 12292 | tf_op jit(solution)/shard_map/while
  107.4 16.0 %all-to-all-start.1 = ((bf16[32,2,32,128]{3,2,1,0:T(8,128)(2,1)}), bf16[32,2,32,128]{3,2,1,0:T(8,128)(2,1)S(1)}, u32[]{:S(2)}, u32[]{:S(2)}) async-start(bf16[32,2,32,128]{3,2,1,0:T(8,128)(2,1)} %select_multiply_fusion.2), calls=%async_computation.1 | async-start | bytes 1048576 | tf_op jit(solution)/shard_map/while/body/eval_jaxpr/all_to_all | solution.py:61
  124.4 21.0 %all-to-all-start = ((bf16[8,8,32,128]{3,2,1,0:T(8,128)(2,1)}), bf16[8,8,32,128]{3,2,1,0:T(8,128)(2,1)S(1)}, u32[]{:S(2)}, u32[]{:S(2)}) async-start(bf16[8,8,32,128]{3,2,1,0:T(8,128)(2,1)} %stack.4), calls=%async_computation | async-start | bytes 1048576 | tf_op jit(solution)/shard_map/while/body/eval_jaxpr/all_to_all | solution.py:41
  146.4 4.5 copy-start
  146.4 4.5 copy-start.1
  146.4 4.5 copy-start.2
  152.3 7.9 %copy-start.4 = (s32[8,32]{1,0:T(8,128)S(1)}, s32[8,32]{1,0:T(8,128)}, u32[]{:S(2)}) copy-start(s32[8,32]{1,0:T(8,128)} %get-tuple-element.279) | copy-start | bytes 3076 | tf_op jit(solution)/shard_map/while
  152.9 22.2 %copy-start.5 = (f32[8,1,128]{2,0,1:T(8,128)S(1)}, f32[8,1,128]{2,0,1:T(8,128)}, u32[]{:S(2)}) copy-start(f32[8,1,128]{2,0,1:T(8,128)} %get-tuple-element.278) | copy-start | bytes 12292 | tf_op jit(solution)/shard_map/while
  153.9 16.1 %all-to-all-start.1 = ((bf16[32,2,32,128]{3,2,1,0:T(8,128)(2,1)}), bf16[32,2,32,128]{3,2,1,0:T(8,128)(2,1)S(1)}, u32[]{:S(2)}, u32[]{:S(2)}) async-start(bf16[32,2,32,128]{3,2,1,0:T(8,128)(2,1)} %select_multiply_fusion.2), calls=%async_computation.1 | async-start | bytes 1048576 | tf_op jit(solution)/shard_map/while/body/eval_jaxpr/all_to_all | solution.py:61
  170.8 21.0 %all-to-all-start = ((bf16[8,8,32,128]{3,2,1,0:T(8,128)(2,1)}), bf16[8,8,32,128]{3,2,1,0:T(8,128)(2,1)S(1)}, u32[]{:S(2)}, u32[]{:S(2)}) async-start(bf16[8,8,32,128]{3,2,1,0:T(8,128)(2,1)} %stack.4), calls=%async_computation | async-start | bytes 1048576 | tf_op jit(solution)/shard_map/while/body/eval_jaxpr/all_to_all | solution.py:41
  192.8 4.5 copy-start
  192.8 4.5 copy-start.1
  192.9 4.5 copy-start.2
  198.7 7.9 %copy-start.4 = (s32[8,32]{1,0:T(8,128)S(1)}, s32[8,32]{1,0:T(8,128)}, u32[]{:S(2)}) copy-start(s32[8,32]{1,0:T(8,128)} %get-tuple-element.279) | copy-start | bytes 3076 | tf_op jit(solution)/shard_map/while
  199.4 22.2 %copy-start.5 = (f32[8,1,128]{2,0,1:T(8,128)S(1)}, f32[8,1,128]{2,0,1:T(8,128)}, u32[]{:S(2)}) copy-start(f32[8,1,128]{2,0,1:T(8,128)} %get-tuple-element.278) | copy-start | bytes 12292 | tf_op jit(solution)/shard_map/while
  200.3 16.1 %all-to-all-start.1 = ((bf16[32,2,32,128]{3,2,1,0:T(8,128)(2,1)}), bf16[32,2,32,128]{3,2,1,0:T(8,128)(2,1)S(1)}, u32[]{:S(2)}, u32[]{:S(2)}) async-start(bf16[32,2,32,128]{3,2,1,0:T(8,128)(2,1)} %select_multiply_fusion.2), calls=%async_computation.1 | async-start | bytes 1048576 | tf_op jit(solution)/shard_map/while/body/eval_jaxpr/all_to_all | solution.py:61
  217.3 21.0 %all-to-all-start = ((bf16[8,8,32,128]{3,2,1,0:T(8,128)(2,1)}), bf16[8,8,32,128]{3,2,1,0:T(8,128)(2,1)S(1)}, u32[]{:S(2)}, u32[]{:S(2)}) async-start(bf16[8,8,32,128]{3,2,1,0:T(8,128)(2,1)} %stack.4), calls=%async_computation | async-start | bytes 1048576 | tf_op jit(solution)/shard_map/while/body/eval_jaxpr/all_to_all | solution.py:41
  239.3 4.5 copy-start
  239.3 4.5 copy-start.1
  239.3 4.5 copy-start.2
  245.1 7.9 %copy-start.4 = (s32[8,32]{1,0:T(8,128)S(1)}, s32[8,32]{1,0:T(8,128)}, u32[]{:S(2)}) copy-start(s32[8,32]{1,0:T(8,128)} %get-tuple-element.279) | copy-start | bytes 3076 | tf_op jit(solution)/shard_map/while
  245.8 22.2 %copy-start.5 = (f32[8,1,128]{2,0,1:T(8,128)S(1)}, f32[8,1,128]{2,0,1:T(8,128)}, u32[]{:S(2)}) copy-start(f32[8,1,128]{2,0,1:T(8,128)} %get-tuple-element.278) | copy-start | bytes 12292 | tf_op jit(solution)/shard_map/while
  246.8 16.1 %all-to-all-start.1 = ((bf16[32,2,32,128]{3,2,1,0:T(8,128)(2,1)}), bf16[32,2,32,128]{3,2,1,0:T(8,128)(2,1)S(1)}, u32[]{:S(2)}, u32[]{:S(2)}) async-start(bf16[32,2,32,128]{3,2,1,0:T(8,128)(2,1)} %select_multiply_fusion.2), calls=%async_computation.1 | async-start | bytes 1048576 | tf_op jit(solution)/shard_map/while/body/eval_jaxpr/all_to_all | solution.py:61
  263.7 21.0 %all-to-all-start = ((bf16[8,8,32,128]{3,2,1,0:T(8,128)(2,1)}), bf16[8,8,32,128]{3,2,1,0:T(8,128)(2,1)S(1)}, u32[]{:S(2)}, u32[]{:S(2)}) async-start(bf16[8,8,32,128]{3,2,1,0:T(8,128)(2,1)} %stack.4), calls=%async_computation | async-start | bytes 1048576 | tf_op jit(solution)/shard_map/while/body/eval_jaxpr/all_to_all | solution.py:41
  285.7 4.5 copy-start
  285.7 4.5 copy-start.1
  285.7 4.5 copy-start.2
  291.6 7.9 %copy-start.4 = (s32[8,32]{1,0:T(8,128)S(1)}, s32[8,32]{1,0:T(8,128)}, u32[]{:S(2)}) copy-start(s32[8,32]{1,0:T(8,128)} %get-tuple-element.279) | copy-start | bytes 3076 | tf_op jit(solution)/shard_map/while
  292.3 22.2 %copy-start.5 = (f32[8,1,128]{2,0,1:T(8,128)S(1)}, f32[8,1,128]{2,0,1:T(8,128)}, u32[]{:S(2)}) copy-start(f32[8,1,128]{2,0,1:T(8,128)} %get-tuple-element.278) | copy-start | bytes 12292 | tf_op jit(solution)/shard_map/while
  293.2 16.1 %all-to-all-start.1 = ((bf16[32,2,32,128]{3,2,1,0:T(8,128)(2,1)}), bf16[32,2,32,128]{3,2,1,0:T(8,128)(2,1)S(1)}, u32[]{:S(2)}, u32[]{:S(2)}) async-start(bf16[32,2,32,128]{3,2,1,0:T(8,128)(2,1)} %select_multiply_fusion.2), calls=%async_computation.1 | async-start | bytes 1048576 | tf_op jit(solution)/shard_map/while/body/eval_jaxpr/all_to_all | solution.py:61
  310.1 21.0 %all-to-all-start = ((bf16[8,8,32,128]{3,2,1,0:T(8,128)(2,1)}), bf16[8,8,32,128]{3,2,1,0:T(8,128)(2,1)S(1)}, u32[]{:S(2)}, u32[]{:S(2)}) async-start(bf16[8,8,32,128]{3,2,1,0:T(8,128)(2,1)} %stack.4), calls=%async_computation | async-start | bytes 1048576 | tf_op jit(solution)/shard_map/while/body/eval_jaxpr/all_to_all | solution.py:41
  332.2 4.5 copy-start
  332.2 4.5 copy-start.1
  332.2 4.5 copy-start.2
  338.0 7.9 %copy-start.4 = (s32[8,32]{1,0:T(8,128)S(1)}, s32[8,32]{1,0:T(8,128)}, u32[]{:S(2)}) copy-start(s32[8,32]{1,0:T(8,128)} %get-tuple-element.279) | copy-start | bytes 3076 | tf_op jit(solution)/shard_map/while
  338.7 22.2 %copy-start.5 = (f32[8,1,128]{2,0,1:T(8,128)S(1)}, f32[8,1,128]{2,0,1:T(8,128)}, u32[]{:S(2)}) copy-start(f32[8,1,128]{2,0,1:T(8,128)} %get-tuple-element.278) | copy-start | bytes 12292 | tf_op jit(solution)/shard_map/while
  339.7 16.1 %all-to-all-start.1 = ((bf16[32,2,32,128]{3,2,1,0:T(8,128)(2,1)}), bf16[32,2,32,128]{3,2,1,0:T(8,128)(2,1)S(1)}, u32[]{:S(2)}, u32[]{:S(2)}) async-start(bf16[32,2,32,128]{3,2,1,0:T(8,128)(2,1)} %select_multiply_fusion.2), calls=%async_computation.1 | async-start | bytes 1048576 | tf_op jit(solution)/shard_map/while/body/eval_jaxpr/all_to_all | solution.py:61
  356.6 21.0 %all-to-all-start = ((bf16[8,8,32,128]{3,2,1,0:T(8,128)(2,1)}), bf16[8,8,32,128]{3,2,1,0:T(8,128)(2,1)S(1)}, u32[]{:S(2)}, u32[]{:S(2)}) async-start(bf16[8,8,32,128]{3,2,1,0:T(8,128)(2,1)} %stack.4), calls=%async_computation | async-start | bytes 1048576 | tf_op jit(solution)/shard_map/while/body/eval_jaxpr/all_to_all | solution.py:41
  378.6 4.5 copy-start
  378.6 4.5 copy-start.1
  378.6 4.5 copy-start.2
  384.5 7.9 %copy-start.4 = (s32[8,32]{1,0:T(8,128)S(1)}, s32[8,32]{1,0:T(8,128)}, u32[]{:S(2)}) copy-start(s32[8,32]{1,0:T(8,128)} %get-tuple-element.279) | copy-start | bytes 3076 | tf_op jit(solution)/shard_map/while
  385.2 22.2 %copy-start.5 = (f32[8,1,128]{2,0,1:T(8,128)S(1)}, f32[8,1,128]{2,0,1:T(8,128)}, u32[]{:S(2)}) copy-start(f32[8,1,128]{2,0,1:T(8,128)} %get-tuple-element.278) | copy-start | bytes 12292 | tf_op jit(solution)/shard_map/while
  386.1 16.1 %all-to-all-start.1 = ((bf16[32,2,32,128]{3,2,1,0:T(8,128)(2,1)}), bf16[32,2,32,128]{3,2,1,0:T(8,128)(2,1)S(1)}, u32[]{:S(2)}, u32[]{:S(2)}) async-start(bf16[32,2,32,128]{3,2,1,0:T(8,128)(2,1)} %select_multiply_fusion.2), calls=%async_computation.1 | async-start | bytes 1048576 | tf_op jit(solution)/shard_map/while/body/eval_jaxpr/all_to_all | solution.py:61
  403.0 21.0 %all-to-all-start = ((bf16[8,8,32,128]{3,2,1,0:T(8,128)(2,1)}), bf16[8,8,32,128]{3,2,1,0:T(8,128)(2,1)S(1)}, u32[]{:S(2)}, u32[]{:S(2)}) async-start(bf16[8,8,32,128]{3,2,1,0:T(8,128)(2,1)} %stack.4), calls=%async_computation | async-start | bytes 1048576 | tf_op jit(solution)/shard_map/while/body/eval_jaxpr/all_to_all | solution.py:41
  425.0 4.5 copy-start
  425.1 4.5 copy-start.1
  425.1 4.5 copy-start.2
  430.9 7.9 %copy-start.4 = (s32[8,32]{1,0:T(8,128)S(1)}, s32[8,32]{1,0:T(8,128)}, u32[]{:S(2)}) copy-start(s32[8,32]{1,0:T(8,128)} %get-tuple-element.279) | copy-start | bytes 3076 | tf_op jit(solution)/shard_map/while
  431.6 22.2 %copy-start.5 = (f32[8,1,128]{2,0,1:T(8,128)S(1)}, f32[8,1,128]{2,0,1:T(8,128)}, u32[]{:S(2)}) copy-start(f32[8,1,128]{2,0,1:T(8,128)} %get-tuple-element.278) | copy-start | bytes 12292 | tf_op jit(solution)/shard_map/while
  432.5 16.1 %all-to-all-start.1 = ((bf16[32,2,32,128]{3,2,1,0:T(8,128)(2,1)}), bf16[32,2,32,128]{3,2,1,0:T(8,128)(2,1)S(1)}, u32[]{:S(2)}, u32[]{:S(2)}) async-start(bf16[32,2,32,128]{3,2,1,0:T(8,128)(2,1)} %select_multiply_fusion.2), calls=%async_computation.1 | async-start | bytes 1048576 | tf_op jit(solution)/shard_map/while/body/eval_jaxpr/all_to_all | solution.py:61
  449.5 21.0 %all-to-all-start = ((bf16[8,8,32,128]{3,2,1,0:T(8,128)(2,1)}), bf16[8,8,32,128]{3,2,1,0:T(8,128)(2,1)S(1)}, u32[]{:S(2)}, u32[]{:S(2)}) async-start(bf16[8,8,32,128]{3,2,1,0:T(8,128)(2,1)} %stack.4), calls=%async_computation | async-start | bytes 1048576 | tf_op jit(solution)/shard_map/while/body/eval_jaxpr/all_to_all | solution.py:41
  471.5 4.5 copy-start
  (16 other events, 33.5 us)
